TPU v7x, 256 devices: a whole 4x4x8 slice. The times are simulated.
256 devices in a mesh: row: 16 (over z_hi, y, core), col: 16 (over x, z_lo).
Axes of the slice: x: 4, y: 4, z: 8 (z_hi: 2, z_lo: 4; z = z_hi * 4 + z_lo), core: 2. Of those that a mesh axis runs over, the one named last changes fastest.
Arguments:
- cost_rough: bfloat16 [33792, 33792], P('row', 'col'), may hold values from 0.0009994507 to 1
- land_mask: int32 [176, 192], P('row', 'col'), may hold values 0 or 1
- wage_start: float32 [176, 192, 256], P('row', 'col'), may hold values from -3 to 3
- tech_start: float32 [176, 192, 256], P('row', 'col'), may hold values from -3 to 3
- temp_start: float32 [176, 192, 256], P('row', 'col'), may hold values from -2.5 to 2.5
- damping: float32 [1], replicated, may hold values from 0.3 to 0.8
Outputs:
- wage_field: float32 [176, 192, 256], P('row', 'col')
- tech_field: float32 [176, 192, 256], P('row', 'col')
- temp_field: float32 [176, 192, 256], P('row', 'col')
All inputs are finite; a program needn't handle non-finite values. No bound on the sum of `land_mask` on one device may be relied on, other than what follows from the above.
Results may differ from a plain program's by a relative error of at most 0.0003.
Values may be sent and summed in bfloat16 or wider, within the bound.
A program may use at most 128 MiB of HBM per device.

v0:
```python
import jax
import jax.numpy as jnp
from jax import lax
from jax.sharding import PartitionSpec as P

LAT = 176
LON = 192
ITERS = 3
ELL = 44


def padded_2(cells, sides, width):
    for axis, dim in sides:
        count = lax.axis_size(axis)
        ends = count - 1
        head = lax.slice_in_dim(cells, 0, width, axis=dim)
        tail = lax.slice_in_dim(cells, cells.shape[dim] - width, cells.shape[dim], axis=dim)
        cells = jnp.concatenate(
            [
                lax.ppermute(tail, axis, [(i, (i + 1) % count) for i in range(ends)]),
                cells,
                lax.ppermute(head, axis, [((i + 1) % count, i) for i in range(ends)]),
            ],
            axis=dim,
        )
    return cells


def cost_block(rough_block, destin, source):
    distance = (
        jnp.abs(destin[:, None] // LON - source[None, :] % LAT)
        + jnp.abs(destin[:, None] % LON - source[None, :] // LAT)
    ).astype(jnp.float32)
    scaled = rough_block.astype(jnp.float32) * jnp.exp(-distance / ELL) / (ELL * ELL)
    return scaled.astype(jnp.bfloat16)


def laplace(padded, field):
    return padded[2:, 1:-1] + padded[:-2, 1:-1] + padded[1:-1, 2:] + padded[1:-1, :-2] - 4.0 * field


def local(cost_rough, land_mask, wage_start, tech_start, temp_start, damping):
    height, breadth = cost_rough.shape
    band_lat, band_lon, scenarios = wage_start.shape
    source = lax.axis_index("col") * breadth + jnp.arange(breadth, dtype=jnp.int32)
    lat_first = lax.axis_index("row") * band_lat

    def build_row(pair):
        rough_row, lat_offset = pair
        destin = (lat_first + lat_offset) * LON + jnp.arange(LON, dtype=jnp.int32)
        return cost_block(rough_row, destin, source)

    slabs = lax.map(
        build_row,
        (cost_rough.reshape(band_lat, LON, breadth), jnp.arange(band_lat, dtype=jnp.int32)),
    )
    cost_tile = slabs.reshape(height, breadth)
    share = 0.25 + land_mask.astype(jnp.float32)[:, :, None]
    wage_field, tech_field, temp_field = (wage_start, tech_start, temp_start)
    for iteration in range(ITERS):
        supply = (jnp.exp(tech_field - wage_field) * share).astype(jnp.bfloat16)
        gathered = lax.all_gather(supply, "row", axis=0, tiled=True)
        columns = gathered.transpose(1, 0, 2).reshape(breadth, scenarios)
        product = jnp.dot(cost_tile, columns, preferred_element_type=jnp.float32).reshape(
            band_lat, LON, scenarios
        )
        access = lax.psum_scatter(product, "col", scatter_dimension=1, tiled=True)
        target = 0.5 * (jnp.log(access) + tech_field)
        wage_field = wage_field + damping[0] * (target - wage_field)
        stacked = jnp.stack((tech_field, temp_field))
        padded = padded_2(stacked, (("row", 1), ("col", 2)), 1)
        tech_next = (
            tech_field + 0.2 * laplace(padded[0], tech_field) - 0.05 * temp_field * temp_field
        )
        temp_next = (
            temp_field + 0.2 * laplace(padded[1], temp_field) + 0.5 * share * jnp.tanh(wage_field)
        )
        tech_field, temp_field = (tech_next, temp_next)
    return (wage_field, tech_field, temp_field)


def solution(mesh):
    in_specs = (
        P("row", "col"),
        P("row", "col"),
        P("row", "col", None),
        P("row", "col", None),
        P("row", "col", None),
        P(),
    )
    out_specs = (P("row", "col", None), P("row", "col", None), P("row", "col", None))
    return jax.shard_map(local, mesh=mesh, in_specs=in_specs, out_specs=out_specs, check_vma=False)
```

profile of v0, /device:TPU:24, one launch (start us, length us, event | category | flops | bytes accessed | tf_op | source)
XLA Modules:
  0.0 748.9 jit_solution(5490739183297818805)
XLA Ops:
  7.9 1.7 multiply_convert_fusion.3
  9.8 47.7 %while.15 = (s32[]{:T(128)}, bf16[11,192,2112]{2,1,0:T(8,128)(2,1)}, bf16[11,192,2112]{2,1,0:T(8,128)(2,1)}, s32[11]{0:T(128)S(1)}, s32[]{:T(128)}, /*index=5*/s32[]{:T(128)}, s32[]{:T(128)}, s32[]{:T(128)}) while((s32[]{:T(128)}, bf16[11,192,2112]{2,1,0:T(8,128)(2,1)}, bf16[11,192,2112]{2,1,0:T(8,128)(2,1)}, ...), condition=%wide.region_1.2_spmd.clone.clone, body=%wide.region_0.1_spmd.clone.clone.sunk | while | flops 4898116 | bytes 1712901 | solution.py:53
  11.0 3.1 fusion.66
  15.3 3.1 fusion.66
  19.7 3.1 fusion.66
  24.0 3.0 fusion.66
  28.3 3.1 fusion.66
  32.6 3.1 fusion.66
  37.0 3.1 fusion.66
  41.3 3.1 fusion.66
  45.6 3.1 fusion.66
  49.9 3.1 fusion.66
  54.3 3.1 fusion.66
  57.4 14.5 %all-gather.4.cloned.1.call-done = bf16[176,12,256]{2,1,0:T(8,128)(2,1)} async-done(((bf16[11,12,256]{2,1,0:T(8,128)(2,1)}), bf16[176,12,256]{2,1,0:T(8,128)(2,1)}) %all-gather.4.cloned.1.call-update) | async-done | bytes 1081360 | tf_op jit(solution)/shard_map/all_gather | solution.py:62
  71.9 1.7 copy.13
  73.7 7.8 %fusion.56 = f32[11,192,256]{2,1,0:T(8,128)} fusion(bf16[11,192,2112]{2,1,0:T(8,128)(2,1)} %get-tuple-element.124, bf16[2112,256,1]{1,0,2:T(8,128)(2,1)S(1)} %bitcast.73), kind=kOutput, calls=%fused_computation.113 | convolution fusion | flops 2283798528 | bytes 12165120 | tf_op jit(solution)/shard_map/dot_general | solution.py:64
  81.5 0.8 copy-done
  82.5 2.1 collective-permute-start
  84.6 3.4 collective-permute-start.1
  88.0 1.6 collective-permute-done.1
  89.6 1.8 collective-permute-start.2
  91.5 1.3 collective-permute-start.3
  94.7 2.9 collective-permute-done.3
  97.7 157.4 %all-reduce.7.cloned.1.call-done = f32[11,192,256]{2,1,0:T(8,128)} async-done(((f32[11,192,256]{2,1,0:T(8,128)}), f32[11,192,256]{2,1,0:T(8,128)}) %all-reduce.7.cloned.1.call-update) | async-done | bytes 2162704
  255.1 1.1 fusion.32
  256.2 0.8 multiply_convert_fusion.2
  257.1 57.6 %all-gather.6.cloned.1.call-done = bf16[176,12,256]{2,1,0:T(8,128)(2,1)} async-done(((bf16[11,12,256]{2,1,0:T(8,128)(2,1)}), bf16[176,12,256]{2,1,0:T(8,128)(2,1)}) %all-gather.6.cloned.1.call-update) | async-done | bytes 1081360 | tf_op jit(solution)/shard_map/all_gather | solution.py:62
  314.7 1.7 copy.14
  316.4 7.8 %fusion.57 = f32[11,192,256]{2,1,0:T(8,128)} fusion(bf16[11,192,2112]{2,1,0:T(8,128)(2,1)} %get-tuple-element.124, bf16[2112,256,1]{1,0,2:T(8,128)(2,1)S(1)} %bitcast.75), kind=kOutput, calls=%fused_computation.114 | convolution fusion | flops 2283798528 | bytes 12165120 | tf_op jit(solution)/shard_map/dot_general | solution.py:64
  324.3 2.1 collective-permute-start.4
  326.4 3.4 collective-permute-start.5
  329.9 1.6 collective-permute-done.5
  331.5 1.8 collective-permute-start.6
  333.3 1.3 collective-permute-start.7
  334.8 4.6 collective-permute-done.7
  339.6 157.7 %all-reduce.9.cloned.1.call-done = f32[11,192,256]{2,1,0:T(8,128)} async-done(((f32[11,192,256]{2,1,0:T(8,128)}), f32[11,192,256]{2,1,0:T(8,128)}) %all-reduce.9.cloned.1.call-update) | async-done | bytes 2162704
  497.2 1.1 fusion.25
  499.4 57.8 %all-gather.8.cloned.1.call-done = bf16[176,12,256]{2,1,0:T(8,128)(2,1)} async-done(((bf16[11,12,256]{2,1,0:T(8,128)(2,1)}), bf16[176,12,256]{2,1,0:T(8,128)(2,1)}) %all-gather.8.cloned.1.call-update) | async-done | bytes 1081360 | tf_op jit(solution)/shard_map/all_gather | solution.py:62
  557.2 1.7 copy.15
  558.9 7.7 %fusion.58 = f32[11,192,256]{2,1,0:T(8,128)} fusion(bf16[11,192,2112]{2,1,0:T(8,128)(2,1)} %get-tuple-element.124, bf16[2112,256,1]{1,0,2:T(8,128)(2,1)S(1)} %bitcast.74), kind=kOutput, calls=%fused_computation.115 | convolution fusion | flops 2283798528 | bytes 12165120 | tf_op jit(solution)/shard_map/dot_general | solution.py:64
  566.6 2.1 collective-permute-start.8
  568.8 3.4 collective-permute-start.9
  572.2 1.6 collective-permute-done.9
  573.8 1.8 collective-permute-start.10
  575.6 1.3 collective-permute-start.11
  577.2 4.7 collective-permute-done.11
  581.9 158.1 %all-reduce.11.cloned.1.call-done = f32[11,192,256]{2,1,0:T(8,128)} async-done(((f32[11,192,256]{2,1,0:T(8,128)}), f32[11,192,256]{2,1,0:T(8,128)}) %all-reduce.11.cloned.1.call-update) | async-done | bytes 2162704
  740.0 2.0 fusion.18
  (86 shorter events, 11.0 us)
Async XLA Ops:
  7.2 64.8 %all-gather.4.cloned.1.call-start = ((), (), s32[]{:S(2)}) async-start(), calls=%async_computation | async-start | bytes 1531904 | tf_op jit(solution)/shard_map/all_gather | solution.py:62
  9.7 245.4 %all-reduce.7.cloned.1.call-start = ((), (), s32[]{:S(2)}) async-start(), calls=%async_computation.3 | async-start | bytes 4325376
  81.4 0.9 copy-start
  81.4 1.0 copy-start.1
  81.4 12.0 %copy-start.3 = (u32[256]{0:T(256)S(1)}, u32[256]{0:T(256)}, u32[]{:S(2)}) copy-start(u32[256]{0:T(256)} %constant.114) | copy-start | bytes 3076
  81.5 173.7 %copy-start.2 = (f32[11,12,256]{2,1,0:T(8,128)S(1)}, f32[11,12,256]{2,1,0:T(8,128)}, u32[]{:S(2)}) copy-start(f32[11,12,256]{2,1,0:T(8,128)} %param.10) | copy-start | bytes 405508
  81.5 233.2 %all-gather.6.cloned.1.call-start = ((), (), s32[]{:S(2)}) async-start(), calls=%async_computation.1 | async-start | bytes 1531904 | tf_op jit(solution)/shard_map/all_gather | solution.py:62
  82.5 5.6 collective-permute-start
  84.6 5.0 collective-permute-start.1
  89.6 5.0 collective-permute-start.2
  91.5 6.1 collective-permute-start.3
  257.0 240.2 %all-reduce.9.cloned.1.call-start = ((), (), s32[]{:S(2)}) async-start(), calls=%async_computation.4 | async-start | bytes 4325376
  324.2 233.0 %all-gather.8.cloned.1.call-start = ((), (), s32[]{:S(2)}) async-start(), calls=%async_computation.2 | async-start | bytes 1531904 | tf_op jit(solution)/shard_map/all_gather | solution.py:62
  324.3 5.6 collective-permute-start.4
  326.4 5.0 collective-permute-start.5
  331.5 3.3 collective-permute-start.6
  333.3 6.1 collective-permute-start.7
  499.1 240.9 %all-reduce.11.cloned.1.call-start = ((), (), s32[]{:S(2)}) async-start(), calls=%async_computation.5 | async-start | bytes 4325376
  566.6 5.6 collective-permute-start.8
  568.8 5.0 collective-permute-start.9
  573.8 3.3 collective-permute-start.10
  575.6 6.2 collective-permute-start.11
Sparse Core Ops, SparseCore 0:
  11.3 60.6 all-gather.3
  81.6 173.4 all-reduce.6
  258.4 56.2 all-gather.5
  324.3 172.8 all-reduce.8
  500.4 56.7 all-gather.7
  566.7 173.2 all-reduce.10
where the time goes:
time: 750 us; the launch traced here: 749 us
  waiting for transfers between devices  621 us (83%)
  other arithmetic  43.5 us (6%)
  starting transfers between devices  26.4 us (4%)
  matrix products  23.2 us (3%)
  between operations  15.7 us (2%)
  local copies, waits for them, and re-layouts  13.1 us (2%)
    unnamed x9, waiting for transfers between devices  473 us
    all_gather x3, waiting for transfers between devices, local(): gathered = lax.all_gather(supply, 'row', axis=0, tiled=True)  130 us
    dynamic_update_slice x11, other arithmetic, local(): lax.map(build_row, (cost_rough.reshape(band_lat, LON, breadth), jnp.arang...  33.9 us
    dot_general x3, matrix products, local(): jnp.dot(cost_tile, columns, preferred_element_type=jnp.float32)  23.2 us
    ppermute x6, waiting for transfers between devices, padded_2(): lax.ppermute(head, axis, [((i + 1) % count, i) for i in range(ends)])  16.9 us
  transfers between devices with their start and end apart: 18, of which 14 were waited for; matrix products, arithmetic and copies ran while one was open for 6% of the time, Pallas kernels for 0%

commit v1 on v0

--- a/solution.py
+++ b/solution.py
@@ -59,7 +59,9 @@
     wage_field, tech_field, temp_field = (wage_start, tech_start, temp_start)
     for iteration in range(ITERS):
         supply = (jnp.exp(tech_field - wage_field) * share).astype(jnp.bfloat16)
-        gathered = lax.all_gather(supply, "row", axis=0, tiled=True)
+        gathered = jnp.concatenate(
+            lax.all_to_all(jnp.stack([supply] * lax.axis_size("row")), "row", 0, 0), axis=0
+        )
         columns = gathered.transpose(1, 0, 2).reshape(breadth, scenarios)
         product = jnp.dot(cost_tile, columns, preferred_element_type=jnp.float32).reshape(
             band_lat, LON, scenarios

time: 750 us -> 721 us (0.961)
  waiting for transfers between devices: 621 us -> 498 us
  blocking collectives: 0 us -> 85.7 us
  starting transfers between devices: 26.4 us -> 37.5 us
    all_gather x3 -> x0, waiting for transfers between devices: 130 us -> none  [local(): gathered = lax.all_gather(supply, 'row', axis=0, tiled=True)]
    all_to_all x0 -> x2, blocking collectives: none -> 85.7 us  [local(): lax.all_to_all(jnp.stack([supply] * lax.axis_size('row')), 'row', 0, 0)]
    all_to_all x0 -> x1, starting transfers between devices: none -> 11.3 us  [local(): lax.all_to_all(jnp.stack([supply] * lax.axis_size('row')), 'row', 0, 0)]
    ppermute x6, waiting for transfers between devices: 16.9 us -> 27 us  [padded_2(): lax.ppermute(head, axis, [((i + 1) % count, i) for i in range(ends)])]
    unnamed x9 -> x6, waiting for transfers between devices: 473 us -> 471 us
  transfers between devices with their start and end apart: 18 -> 16, of which waited for: 14 -> 11; matrix products, arithmetic and copies ran while one was open for 6% -> 6% of each run, Pallas kernels for 0% -> 0%
where the time goes in v1:
time: 721 us; the launch traced here: 720 us
  waiting for transfers between devices  498 us (69%)
  blocking collectives  85.7 us (12%)
  other arithmetic  41.6 us (6%)
  starting transfers between devices  37.5 us (5%)
  matrix products  23.3 us (3%)
  between operations  15.3 us (2%)
  local copies, waits for them, and re-layouts  10.9 us (2%)
    unnamed x6, waiting for transfers between devices  471 us
    all_to_all x2, blocking collectives, local(): lax.all_to_all(jnp.stack([supply] * lax.axis_size('row')), 'row', 0, 0)  85.7 us
    dynamic_update_slice x11, other arithmetic, local(): lax.map(build_row, (cost_rough.reshape(band_lat, LON, breadth), jnp.arang...  33.9 us
    ppermute x6, waiting for transfers between devices, padded_2(): lax.ppermute(head, axis, [((i + 1) % count, i) for i in range(ends)])  27 us
    dot_general x3, matrix products, local(): jnp.dot(cost_tile, columns, preferred_element_type=jnp.float32)  23.3 us
  transfers between devices with their start and end apart: 16, of which 11 were waited for; matrix products, arithmetic and copies ran while one was open for 6% of the time, Pallas kernels for 0%

profile of v1, /device:TPU:24, one launch (start us, length us, event | category | flops | bytes accessed | tf_op | source)
XLA Modules:
  0.0 719.8 jit_solution(5176384223658942896)
XLA Ops:
  7.2 0.7 convert_add_fusion
  7.9 1.1 multiply_convert_fusion.3
  9.0 1.2 stack.24
  10.2 11.3 %all-to-all-start = ((bf16[16,11,12,256]{3,2,1,0:T(8,128)(2,1)}), bf16[16,11,12,256]{3,2,1,0:T(8,128)(2,1)S(1)}, u32[]{:S(2)}, u32[]{:S(2)}) async-start(bf16[16,11,12,256]{3,2,1,0:T(8,128)(2,1)} %stack.24), calls=%async_computation | async-start | bytes 2883584 | tf_op jit(solution)/shard_map/all_to_all | solution.py:63
  21.6 48.9 %while.15 = (s32[]{:T(128)}, bf16[11,192,2112]{2,1,0:T(8,128)(2,1)}, bf16[11,192,2112]{2,1,0:T(8,128)(2,1)}, s32[11]{0:T(128)S(1)}, s32[]{:T(128)}, /*index=5*/s32[]{:T(128)}, s32[]{:T(128)}, s32[]{:T(128)}) while((s32[]{:T(128)}, bf16[11,192,2112]{2,1,0:T(8,128)(2,1)}, bf16[11,192,2112]{2,1,0:T(8,128)(2,1)}, ...), condition=%wide.region_1.2_spmd.clone.clone, body=%wide.region_0.1_spmd.clone.clone.sunk | while | flops 4898116 | bytes 1712901 | solution.py:53
  21.7 0.6 dynamic_slice.24
  23.0 3.1 fusion.66
  27.4 3.1 fusion.66
  31.8 3.1 fusion.66
  36.3 3.1 fusion.66
  40.7 3.1 fusion.66
  45.1 3.1 fusion.66
  49.5 3.1 fusion.66
  54.0 3.1 fusion.66
  58.4 3.1 fusion.66
  62.8 3.1 fusion.66
  66.0 0.6 dynamic_slice.24
  67.3 3.1 fusion.66
  70.8 7.8 %fusion.56 = f32[11,192,256]{2,1,0:T(8,128)} fusion(bf16[11,192,2112]{2,1,0:T(8,128)(2,1)} %get-tuple-element.124, bf16[2112,256,1]{1,0,2:T(8,128)(2,1)S(1)} %bitcast.79), kind=kOutput, calls=%fused_computation.113 | convolution fusion | flops 2283798528 | bytes 12165120 | tf_op jit(solution)/shard_map/dot_general | solution.py:66
  78.7 0.8 copy-done
  79.6 2.0 collective-permute-start
  81.7 3.5 collective-permute-start.1
  85.2 4.4 collective-permute-done.1
  89.7 2.9 collective-permute-start.2
  92.6 1.3 collective-permute-start.3
  95.8 3.6 collective-permute-done.3
  99.5 157.2 %all-reduce.7.cloned.1.call-done = f32[11,192,256]{2,1,0:T(8,128)} async-done(((f32[11,192,256]{2,1,0:T(8,128)}), f32[11,192,256]{2,1,0:T(8,128)}) %all-reduce.7.cloned.1.call-update) | async-done | bytes 2162704
  256.7 1.1 fusion.32
  258.1 42.7 %all_to_all.15 = bf16[16,11,12,256]{3,2,1,0:T(8,128)(2,1)S(1)} all-to-all(bf16[16,11,12,256]{3,2,1,0:T(8,128)(2,1)S(1)} %stack.28), channel_id=1, replica_groups=mesh['row'=16,'col'=16] {'row'}, dimensions={0} | all-to-all | bytes 2162688 | tf_op jit(solution)/shard_map/all_to_all | solution.py:63
  301.1 7.8 %fusion.57 = f32[11,192,256]{2,1,0:T(8,128)} fusion(bf16[11,192,2112]{2,1,0:T(8,128)(2,1)} %get-tuple-element.124, bf16[2112,256,1]{1,0,2:T(8,128)(2,1)S(1)} %bitcast.81), kind=kOutput, calls=%fused_computation.114 | convolution fusion | flops 2283798528 | bytes 12165120 | tf_op jit(solution)/shard_map/dot_general | solution.py:66
  309.0 2.2 collective-permute-start.4
  311.3 3.4 collective-permute-start.5
  314.6 5.2 collective-permute-done.5
  319.8 1.3 collective-permute-start.6
  321.1 1.3 collective-permute-start.7
  322.6 4.6 collective-permute-done.7
  327.4 156.6 %all-reduce.9.cloned.1.call-done = f32[11,192,256]{2,1,0:T(8,128)} async-done(((f32[11,192,256]{2,1,0:T(8,128)}), f32[11,192,256]{2,1,0:T(8,128)}) %all-reduce.9.cloned.1.call-update) | async-done | bytes 2162704
  484.0 1.1 fusion.25
  485.3 43.0 %all_to_all.16 = bf16[16,11,12,256]{3,2,1,0:T(8,128)(2,1)S(1)} all-to-all(bf16[16,11,12,256]{3,2,1,0:T(8,128)(2,1)S(1)} %stack.32), channel_id=1, replica_groups=mesh['row'=16,'col'=16] {'row'}, dimensions={0} | all-to-all | bytes 2162688 | tf_op jit(solution)/shard_map/all_to_all | solution.py:63
  528.7 7.7 %fusion.58 = f32[11,192,256]{2,1,0:T(8,128)} fusion(bf16[11,192,2112]{2,1,0:T(8,128)(2,1)} %get-tuple-element.124, bf16[2112,256,1]{1,0,2:T(8,128)(2,1)S(1)} %bitcast.80), kind=kOutput, calls=%fused_computation.115 | convolution fusion | flops 2283798528 | bytes 12165120 | tf_op jit(solution)/shard_map/dot_general | solution.py:66
  536.4 2.2 collective-permute-start.8
  538.7 3.4 collective-permute-start.9
  542.0 4.8 collective-permute-done.9
  546.9 1.3 collective-permute-start.10
  548.2 1.3 collective-permute-start.11
  549.7 4.5 collective-permute-done.11
  554.3 157.0 %all-reduce.11.cloned.1.call-done = f32[11,192,256]{2,1,0:T(8,128)} async-done(((f32[11,192,256]{2,1,0:T(8,128)}), f32[11,192,256]{2,1,0:T(8,128)}) %all-reduce.11.cloned.1.call-update) | async-done | bytes 2162704
  711.3 2.0 fusion.18
  (84 shorter events, 9.9 us)
Async XLA Ops:
  10.2 60.3 %all-to-all-start = ((bf16[16,11,12,256]{3,2,1,0:T(8,128)(2,1)}), bf16[16,11,12,256]{3,2,1,0:T(8,128)(2,1)S(1)}, u32[]{:S(2)}, u32[]{:S(2)}) async-start(bf16[16,11,12,256]{3,2,1,0:T(8,128)(2,1)} %stack.24), calls=%async_computation | async-start | bytes 2883584 | tf_op jit(solution)/shard_map/all_to_all | solution.py:63
  21.5 235.2 %all-reduce.7.cloned.1.call-start = ((), (), s32[]{:S(2)}) async-start(), calls=%async_computation.3 | async-start | bytes 4325376
  78.6 0.9 copy-start
  78.6 1.0 copy-start.1
  78.6 15.9 %copy-start.3 = (u32[256]{0:T(256)S(1)}, u32[256]{0:T(256)}, u32[]{:S(2)}) copy-start(u32[256]{0:T(256)} %constant.114) | copy-start | bytes 3076
  78.7 178.1 %copy-start.2 = (f32[11,12,256]{2,1,0:T(8,128)S(1)}, f32[11,12,256]{2,1,0:T(8,128)}, u32[]{:S(2)}) copy-start(f32[11,12,256]{2,1,0:T(8,128)} %param.10) | copy-start | bytes 405508
  78.7 405.3 %all-reduce.9.cloned.1.call-start = ((), (), s32[]{:S(2)}) async-start(), calls=%async_computation.4 | async-start | bytes 4325376
  79.6 5.6 collective-permute-start
  81.7 8.0 %collective-permute-start.1 = (f32[2,1,12,256]{3,2,1,0:T(8,128)S(1)}, f32[2,1,12,256]{3,2,1,0:T(8,128)S(1)}, u32[]{:S(2)}, u32[]{:S(2)}) collective-permute-start(f32[2,1,12,256]{3,2,1,0:T(8,128)S(1)} %get-tuple-element.205), channel_id=1, source_target_pairs={{16,0},{32,16},{48,32},{64,48},{80,64},{96,80},{112,96},{128,112},... | collective-permute-start | bytes 73736 | tf_op jit(solution)/shard_map/ppermute | solution.py:22
  89.7 6.1 collective-permute-start.2
  92.6 6.8 collective-permute-start.3
  309.0 402.3 %all-reduce.11.cloned.1.call-start = ((), (), s32[]{:S(2)}) async-start(), calls=%async_computation.5 | async-start | bytes 4325376
  309.0 5.6 collective-permute-start.4
  311.3 8.5 %collective-permute-start.5 = (f32[2,1,12,256]{3,2,1,0:T(8,128)S(1)}, f32[2,1,12,256]{3,2,1,0:T(8,128)S(1)}, u32[]{:S(2)}, u32[]{:S(2)}) collective-permute-start(f32[2,1,12,256]{3,2,1,0:T(8,128)S(1)} %get-tuple-element.203), channel_id=1, source_target_pairs={{16,0},{32,16},{48,32},{64,48},{80,64},{96,80},{112,96},{128,112},... | collective-permute-start | bytes 73736 | tf_op jit(solution)/shard_map/ppermute | solution.py:22
  319.8 2.8 collective-permute-start.6
  321.1 6.1 collective-permute-start.7
  536.4 5.6 collective-permute-start.8
  538.7 8.2 %collective-permute-start.9 = (f32[2,1,12,256]{3,2,1,0:T(8,128)S(1)}, f32[2,1,12,256]{3,2,1,0:T(8,128)S(1)}, u32[]{:S(2)}, u32[]{:S(2)}) collective-permute-start(f32[2,1,12,256]{3,2,1,0:T(8,128)S(1)} %get-tuple-element.201), channel_id=1, source_target_pairs={{16,0},{32,16},{48,32},{64,48},{80,64},{96,80},{112,96},{128,112},... | collective-permute-start | bytes 73736 | tf_op jit(solution)/shard_map/ppermute | solution.py:22
  546.9 2.8 collective-permute-start.10
  548.2 6.0 collective-permute-start.11
Sparse Core Ops, SparseCore 0:
  78.8 177.9 all-reduce.6
  309.1 174.8 all-reduce.8
  536.5 174.7 all-reduce.10
